TPU v7x, 32 devices: a whole 2x2x4 slice. The times are simulated.
32 devices in a mesh: rows: 16 (over z, y, core), maze: 2 (over x).
Axes of the slice: x: 2, y: 2, z: 4, core: 2. Of those that a mesh axis runs over, the one named last changes fastest.
Arguments:
- maze_walls: int32 [2, 128, 256], P('maze', 'rows'), may hold values 0 or 1
- goal_cell: int32 [2, 2], P('maze'), may hold values from 0 to 127
- start_hidden: bfloat16 [2, 32, 128, 256], P('maze', None, 'rows'), may hold values from -0.8984375 to 0.8984375
- start_cell: float32 [2, 32, 128, 256], P('maze', None, 'rows'), may hold values from -4 to 4
- cotangent: bfloat16 [2, 3, 32, 128, 256], P('maze', None, None, 'rows'), may hold values from -6 to 6
- gate_weights: bfloat16 [73728], P(('rows', 'maze')), may hold values from -0.25 to 0.25
- embed_table: float32 [3, 32], replicated, may hold values from -4 to 4
Outputs:
- grad_weights: float32 [73728], P(('rows', 'maze'))
- grad_table: float32 [3, 32], replicated
- grad_hidden: float32 [2, 32, 128, 256], P('maze', None, 'rows')
- grad_cell: float32 [2, 32, 128, 256], P('maze', None, 'rows')
Inputs may be any that keep to these rules, and one draw needn't show every extreme that they name: `maze_walls`: 0 for open cells, 1 for walls. `goal_cell`: goal row and column inside the grid.
All inputs are finite; a program needn't handle non-finite values. No bound on the sum of `maze_walls` on one device may be relied on, other than what follows from the above.
Results may differ from a plain program's by a relative error of at most 0.0044.
Values may be sent and summed in bfloat16 or wider, within the bound.
A program may use at most 64 MiB of HBM per device.

v0:
```python
import math

import jax
import jax.numpy as jnp
from jax import lax
from jax.sharding import PartitionSpec as P

goal_reach = 64.0


def extended(cells, sides, width):
    for axis, dim in sides:
        count = lax.axis_size(axis)
        ends = count - 1
        head = lax.slice_in_dim(cells, 0, width, axis=dim)
        tail = lax.slice_in_dim(cells, cells.shape[dim] - width, cells.shape[dim], axis=dim)
        cells = jnp.concatenate(
            [
                lax.ppermute(tail, axis, [(i, (i + 1) % count) for i in range(ends)]),
                cells,
                lax.ppermute(head, axis, [((i + 1) % count, i) for i in range(ends)]),
            ],
            axis=dim,
        )
    return cells


def tap_offsets():
    return [(row_off, col_off) for row_off in (-1, 0, 1) for col_off in (-1, 0, 1)]


def gate_conv(padded, kernel, row_count, col_count):
    summed = None
    for tap_index, (row_off, col_off) in enumerate(tap_offsets()):
        window = padded[
            :, 1 + row_off : 1 + row_off + row_count, 1 + col_off : 1 + col_off + col_count
        ]
        tap_term = jnp.einsum(
            "gc,crq->grq", kernel[tap_index], window, preferred_element_type=jnp.float32
        )
        summed = tap_term if summed is None else summed + tap_term
    return summed


def weight_grads(gate_grad, padded, row_count, col_count):
    pieces = []
    for row_off, col_off in tap_offsets():
        window = padded[
            :, 1 + row_off : 1 + row_off + row_count, 1 + col_off : 1 + col_off + col_count
        ]
        pieces.append(
            jnp.einsum("grq,crq->gc", gate_grad, window, preferred_element_type=jnp.float32)
        )
    return jnp.stack(pieces)


def per_device(
    maze_walls, goal_cell, start_hidden, start_cell, cotangent, gate_weights, embed_table
):
    row_count = maze_walls.shape[1]
    col_count = maze_walls.shape[2]
    hidden_width = start_hidden.shape[1]
    input_width = embed_table.shape[1]
    channels = input_width + hidden_width
    step_count = cotangent.shape[1]
    gathered = lax.all_gather(gate_weights, ("rows", "maze"), axis=0, tiled=True)
    kernel = gathered.reshape(9, 4 * hidden_width, channels)
    first_row = lax.axis_index("rows") * row_count
    row_pos = first_row + lax.broadcasted_iota(jnp.int32, (row_count, col_count), 0)
    col_pos = lax.broadcasted_iota(jnp.int32, (row_count, col_count), 1)
    distance = (jnp.abs(row_pos - goal_cell[0, 0]) + jnp.abs(col_pos - goal_cell[0, 1])).astype(
        jnp.float32
    )
    goal_bump = jnp.exp(-distance / goal_reach)
    wall_mask = (maze_walls[0] == 1).astype(jnp.float32)
    inputs = (
        embed_table[0][:, None, None] * (1.0 - wall_mask)
        + embed_table[1][:, None, None] * wall_mask
        + embed_table[2][:, None, None] * goal_bump
    ).astype(jnp.bfloat16)
    input_ext = extended(inputs, (("rows", 1),), 1)
    hidden = start_hidden[0]
    cell_state = start_cell[0]
    stored = []
    for step_index in range(step_count):
        hidden_ext = extended(hidden, (("rows", 1),), 1)
        padded = jnp.pad(jnp.concatenate([input_ext, hidden_ext], axis=0), ((0, 0), (0, 0), (1, 1)))
        pre_gate = gate_conv(padded, kernel, row_count, col_count)
        in_gate = jax.nn.sigmoid(pre_gate[:hidden_width])
        forget_gate = jax.nn.sigmoid(pre_gate[hidden_width : 2 * hidden_width] + 1.0)
        out_gate = jax.nn.sigmoid(pre_gate[2 * hidden_width : 3 * hidden_width])
        cand_gate = jnp.tanh(pre_gate[3 * hidden_width :])
        new_cell = forget_gate * cell_state + in_gate * cand_gate
        squash = jnp.tanh(new_cell)
        stored.append((padded, cell_state, in_gate, forget_gate, out_gate, cand_gate, squash))
        hidden = (out_gate * squash).astype(jnp.bfloat16)
        cell_state = new_cell
    carry_hidden = jnp.zeros((hidden_width, row_count, col_count), jnp.float32)
    carry_cell = jnp.zeros((hidden_width, row_count, col_count), jnp.float32)
    kernel_acc = jnp.zeros((9, 4 * hidden_width, channels), jnp.float32)
    input_acc = jnp.zeros((input_width, row_count, col_count), jnp.float32)
    for step_index in reversed(range(step_count)):
        padded, prev_cell, in_gate, forget_gate, out_gate, cand_gate, squash = stored[step_index]
        hid_grad = cotangent[0, step_index].astype(jnp.float32) + carry_hidden
        cell_grad = carry_cell + hid_grad * out_gate * (1.0 - squash * squash)
        gate_grad = jnp.concatenate(
            [
                cell_grad * cand_gate * in_gate * (1.0 - in_gate),
                cell_grad * prev_cell * forget_gate * (1.0 - forget_gate),
                hid_grad * squash * out_gate * (1.0 - out_gate),
                cell_grad * in_gate * (1.0 - cand_gate * cand_gate),
            ],
            axis=0,
        ).astype(jnp.bfloat16)
        step_kernel = weight_grads(gate_grad, padded, row_count, col_count)
        kernel_acc = kernel_acc + step_kernel
        grad_ext = extended(gate_grad, (("rows", 1),), 1)
        grad_padded = jnp.pad(grad_ext, ((0, 0), (0, 0), (1, 1)))
        stack_grad = None
        for tap_index, (row_off, col_off) in enumerate(tap_offsets()):
            window = grad_padded[
                :, 1 - row_off : 1 - row_off + row_count, 1 - col_off : 1 - col_off + col_count
            ]
            tap_term = jnp.einsum(
                "gc,grq->crq", kernel[tap_index], window, preferred_element_type=jnp.float32
            )
            stack_grad = tap_term if stack_grad is None else stack_grad + tap_term
        input_acc = input_acc + stack_grad[:input_width]
        carry_hidden = stack_grad[input_width:]
        carry_cell = cell_grad * forget_gate
    scale = 1.0 / math.sqrt(
        lax.axis_size("maze") * lax.axis_size("rows") * row_count * col_count * step_count
    )
    grad_weights = (
        lax.psum_scatter(kernel_acc.reshape(-1), ("rows", "maze"), scatter_dimension=0, tiled=True)
        * scale
    )
    pieces = jnp.stack(
        [
            jnp.sum(input_acc * (1.0 - wall_mask), axis=(1, 2)),
            jnp.sum(input_acc * wall_mask, axis=(1, 2)),
            jnp.sum(input_acc * goal_bump, axis=(1, 2)),
        ]
    )
    grad_table = lax.psum(pieces, ("rows", "maze")) * scale
    return (grad_weights, grad_table, carry_hidden[None], carry_cell[None])


def solution(mesh):
    return jax.shard_map(
        per_device,
        mesh=mesh,
        in_specs=(
            P("maze", "rows", None),
            P("maze", None),
            P("maze", None, "rows", None),
            P("maze", None, "rows", None),
            P("maze", None, None, "rows", None),
            P(("rows", "maze")),
            P(),
        ),
        out_specs=(
            P(("rows", "maze")),
            P(),
            P("maze", None, "rows", None),
            P("maze", None, "rows", None),
        ),
        check_vma=False,
    )
```

profile of v0, /device:TPU:0, one launch (start us, length us, event | category | flops | bytes accessed | tf_op | source)
XLA Modules:
  0.0 295.6 jit_solution(9705465087397272263)
XLA Ops:
  7.2 1.3 fusion.286
  11.6 2.4 collective-permute-start
  13.9 1.3 collective-permute-start.1
  16.2 5.2 %collective-permute-start.2 = (bf16[32,1,256]{2,0,1:T(8,128)(2,1)S(1)}, bf16[32,1,256]{2,0,1:T(8,128)(2,1)S(1)}, u32[]{:S(2)}, u32[]{:S(2)}) collective-permute-start(bf16[32,1,256]{2,0,1:T(8,128)(2,1)S(1)} %get-tuple-element.68), channel_id=1, source_target_pairs={{0,2},{2,4},{4,6},{6,8},{8,10},{10,12},{12,14},{14,16},{16,18},{18... | collective-permute-start | bytes 49160 | tf_op jit(solution)/shard_map/ppermute | solution.py:19
  21.4 1.3 collective-permute-start.3
  23.4 71.2 %all-gather = bf16[32,1,2304]{2,1,0:T(2,128)(2,1)S(1)} all-gather(bf16[1,1,2304]{2,1,0:T(2,128)(2,1)S(1)} %reshape.144), channel_id=1, replica_groups=mesh['rows'=16,'maze'=2] {'rows','maze'}, dimensions={0}, use_global_device_ids=true | all-gather | bytes 152064 | tf_op jit(solution)/shard_map/all_gather | solution.py:66
  100.5 1.3 collective-permute-start.4
  101.8 1.3 collective-permute-start.5
  103.1 1.8 collective-permute-done.5
  108.9 1.3 fusion.282
  110.3 2.7 collective-permute-start.6
  112.9 1.3 collective-permute-start.7
  115.0 1.4 collective-permute-done.7
  116.3 0.9 maximum_maximum_fusion.2
  117.3 1.1 fusion.180
  123.8 3.3 %collective-permute-start.8 = (bf16[128,1,256]{2,0,1:T(8,128)(2,1)S(1)}, bf16[128,1,256]{2,0,1:T(8,128)(2,1)S(1)}, u32[]{:S(2)}, u32[]{:S(2)}) collective-permute-start(bf16[128,1,256]{2,0,1:T(8,128)(2,1)S(1)} %get-tuple-element.48), channel_id=1, source_target_pairs={{0,2},{2,4},{4,6},{6,8},{8,10},{10,12},{12,14},{14,16},{16,18},{18... | collective-permute-start | bytes 196616 | tf_op jit(solution)/shard_map/ppermute | solution.py:19
  127.2 1.5 collective-permute-start.9
  136.8 3.3 %collective-permute-start.10 = (bf16[128,1,256]{2,0,1:T(8,128)(2,1)S(1)}, bf16[128,1,256]{2,0,1:T(8,128)(2,1)S(1)}, u32[]{:S(2)}, u32[]{:S(2)}) collective-permute-start(bf16[128,1,256]{2,0,1:T(8,128)(2,1)S(1)} %get-tuple-element.46), channel_id=1, source_target_pairs={{0,2},{2,4},{4,6},{6,8},{8,10},{10,12},{12,14},{14,16},{16,18},{18... | collective-permute-start | bytes 196616 | tf_op jit(solution)/shard_map/ppermute | solution.py:19
  140.2 1.3 collective-permute-start.11
  149.9 4.5 %collective-permute-start.12 = (bf16[128,1,256]{2,0,1:T(8,128)(2,1)S(1)}, bf16[128,1,256]{2,0,1:T(8,128)(2,1)S(1)}, u32[]{:S(2)}, u32[]{:S(2)}) collective-permute-start(bf16[128,1,256]{2,0,1:T(8,128)(2,1)S(1)} %get-tuple-element.44), channel_id=1, source_target_pairs={{0,2},{2,4},{4,6},{6,8},{8,10},{10,12},{12,14},{14,16},{16,18},{18... | collective-permute-start | bytes 196616 | tf_op jit(solution)/shard_map/ppermute | solution.py:19
  154.3 1.5 collective-permute-start.13
  166.8 40.0 %psum.7 = f32[3,32]{1,0:T(4,128)S(1)} all-reduce(f32[3,32]{1,0:T(4,128)S(1)} %pad_maximum_fusion.10), channel_id=1, replica_groups=mesh['rows'=16,'maze'=2] {'rows','maze'}, use_global_device_ids=true, to_apply=%region_4.5 | all-reduce | flops 96 | bytes 768 | tf_op jit(solution)/shard_map/psum | solution.py:145
  207.3 80.1 %all-reduce.9.cloned.1.call-done = f32[73728]{0:T(1024)} async-done(((f32[73728]{0:T(1024)}), f32[73728]{0:T(1024)}) %all-reduce.9.cloned.1.call-update) | async-done | bytes 294928
  287.4 1.4 dynamic-slice_multiply_fusion
  (202 shorter events, 48.2 us)
Async XLA Ops:
  7.2 280.2 %all-reduce.9.cloned.1.call-start = ((), (), s32[]{:S(2)}) async-start(), calls=%async_computation | async-start | bytes 589824
  10.7 12.0 %copy-start.25 = (f32[8,256]{1,0:T(8,128)}, f32[8,256]{1,0:T(8,128)S(1)}, u32[]{:S(2)}) copy-start(f32[8,256]{1,0:T(8,128)S(1)} %get-tuple-element.30) | copy-start | bytes 24580
  10.7 12.0 %copy-start.23 = (f32[8,256]{1,0:T(8,128)}, f32[8,256]{1,0:T(8,128)S(1)}, u32[]{:S(2)}) copy-start(f32[8,256]{1,0:T(8,128)S(1)} %convert_bitcast_fusion) | copy-start | bytes 24580
  11.4 11.3 %copy-start.27 = (f32[8,256]{1,0:T(8,128)}, f32[8,256]{1,0:T(8,128)S(1)}, u32[]{:S(2)}) copy-start(f32[8,256]{1,0:T(8,128)S(1)} %multiply_exponential_fusion) | copy-start | bytes 24580
  11.6 84.9 %collective-permute-start = (bf16[32,1,256]{2,0,1:T(8,128)(2,1)S(1)}, bf16[32,1,256]{2,0,1:T(8,128)(2,1)S(1)}, u32[]{:S(2)}, u32[]{:S(2)}) collective-permute-start(bf16[32,1,256]{2,0,1:T(8,128)(2,1)S(1)} %get-tuple-element.66), channel_id=1, source_target_pairs={{0,2},{2,4},{4,6},{6,8},{8,10},{10,12},{12,14},{14,16},{16,18},{18... | collective-permute-start | bytes 49160 | tf_op jit(solution)/shard_map/ppermute | solution.py:19
  13.9 82.5 %collective-permute-start.1 = (bf16[32,1,256]{2,0,1:T(8,128)(2,1)S(1)}, bf16[32,1,256]{2,0,1:T(8,128)(2,1)S(1)}, u32[]{:S(2)}, u32[]{:S(2)}) collective-permute-start(bf16[32,1,256]{2,0,1:T(8,128)(2,1)S(1)} %get-tuple-element.67), channel_id=1, source_target_pairs={{2,0},{4,2},{6,4},{8,6},{10,8},{12,10},{14,12},{16,14},{18,16},{20... | collective-permute-start | bytes 49160 | tf_op jit(solution)/shard_map/ppermute | solution.py:21
  16.2 80.3 %collective-permute-start.2 = (bf16[32,1,256]{2,0,1:T(8,128)(2,1)S(1)}, bf16[32,1,256]{2,0,1:T(8,128)(2,1)S(1)}, u32[]{:S(2)}, u32[]{:S(2)}) collective-permute-start(bf16[32,1,256]{2,0,1:T(8,128)(2,1)S(1)} %get-tuple-element.68), channel_id=1, source_target_pairs={{0,2},{2,4},{4,6},{6,8},{8,10},{10,12},{12,14},{14,16},{16,18},{18... | collective-permute-start | bytes 49160 | tf_op jit(solution)/shard_map/ppermute | solution.py:19
  21.4 75.1 %collective-permute-start.3 = (bf16[32,1,256]{2,0,1:T(8,128)(2,1)S(1)}, bf16[32,1,256]{2,0,1:T(8,128)(2,1)S(1)}, u32[]{:S(2)}, u32[]{:S(2)}) collective-permute-start(bf16[32,1,256]{2,0,1:T(8,128)(2,1)S(1)} %get-tuple-element.69), channel_id=1, source_target_pairs={{2,0},{4,2},{6,4},{8,6},{10,8},{12,10},{14,12},{16,14},{18,16},{20... | collective-permute-start | bytes 49160 | tf_op jit(solution)/shard_map/ppermute | solution.py:21
  95.8 11.5 %copy-start.7 = (bf16[128,64]{1,0:T(8,128)(2,1)}, bf16[128,64]{1,0:T(8,128)(2,1)S(1)}, u32[]{:S(2)}) copy-start(bf16[128,64]{1,0:T(8,128)(2,1)S(1)} %slice.531) | copy-start | bytes 49156
  96.1 10.2 %copy-start.9 = (bf16[128,64]{1,0:T(8,128)(2,1)}, bf16[128,64]{1,0:T(8,128)(2,1)S(1)}, u32[]{:S(2)}) copy-start(bf16[128,64]{1,0:T(8,128)(2,1)S(1)} %slice.522) | copy-start | bytes 49156
  96.3 9.3 %copy-start = (bf16[128,64]{1,0:T(8,128)(2,1)}, bf16[128,64]{1,0:T(8,128)(2,1)S(1)}, u32[]{:S(2)}) copy-start(bf16[128,64]{1,0:T(8,128)(2,1)S(1)} %slice.516) | copy-start | bytes 49156
  96.4 8.5 %copy-start.2 = (bf16[128,64]{1,0:T(8,128)(2,1)}, bf16[128,64]{1,0:T(8,128)(2,1)S(1)}, u32[]{:S(2)}) copy-start(bf16[128,64]{1,0:T(8,128)(2,1)S(1)} %slice.510) | copy-start | bytes 49156
  96.5 8.4 %copy-start.22 = (bf16[32,1,256]{2,0,1:T(8,128)(2,1)}, bf16[32,1,256]{2,0,1:T(8,128)(2,1)S(1)}, u32[]{:S(2)}) copy-start(bf16[32,1,256]{2,0,1:T(8,128)(2,1)S(1)} %collective-permute-done.1) | copy-start | bytes 49156
  100.5 2.6 collective-permute-start.4
  101.8 3.1 %collective-permute-start.5 = (bf16[32,1,256]{2,0,1:T(8,128)(2,1)S(1)}, bf16[32,1,256]{2,0,1:T(8,128)(2,1)S(1)}, u32[]{:S(2)}, u32[]{:S(2)}) collective-permute-start(bf16[32,1,256]{2,0,1:T(8,128)(2,1)S(1)} %get-tuple-element.65), channel_id=1, source_target_pairs={{2,0},{4,2},{6,4},{8,6},{10,8},{12,10},{14,12},{16,14},{18,16},{20... | collective-permute-start | bytes 49160 | tf_op jit(solution)/shard_map/ppermute | solution.py:21
  108.0 6.2 %copy-start.21 = (bf16[1,3,32,8,256]{4,3,2,1,0:T(8,128)(2,1)S(1)}, bf16[1,3,32,8,256]{4,3,2,1,0:T(8,128)(2,1)}, u32[]{:S(2)}) copy-start(bf16[1,3,32,8,256]{4,3,2,1,0:T(8,128)(2,1)} %param.11) | copy-start | bytes 1179652
  110.3 4.7 %collective-permute-start.6 = (bf16[32,1,256]{2,0,1:T(8,128)(2,1)}, bf16[32,1,256]{2,0,1:T(8,128)(2,1)}, u32[]{:S(2)}, u32[]{:S(2)}) collective-permute-start(bf16[32,1,256]{2,0,1:T(8,128)(2,1)} %get-tuple-element.62), channel_id=1, source_target_pairs={{0,2},{2,4},{4,6},{6,8},{8,10},{10,12},{12,14},{14,16},{16,18},{18... | collective-permute-start | bytes 49160 | tf_op jit(solution)/shard_map/ppermute | solution.py:19
  112.9 3.4 %collective-permute-start.7 = (bf16[32,1,256]{2,0,1:T(8,128)(2,1)}, bf16[32,1,256]{2,0,1:T(8,128)(2,1)}, u32[]{:S(2)}, u32[]{:S(2)}) collective-permute-start(bf16[32,1,256]{2,0,1:T(8,128)(2,1)} %get-tuple-element.63), channel_id=1, source_target_pairs={{2,0},{4,2},{6,4},{8,6},{10,8},{12,10},{14,12},{16,14},{18,16},{20... | collective-permute-start | bytes 49160 | tf_op jit(solution)/shard_map/ppermute | solution.py:21
  123.8 7.5 %collective-permute-start.8 = (bf16[128,1,256]{2,0,1:T(8,128)(2,1)S(1)}, bf16[128,1,256]{2,0,1:T(8,128)(2,1)S(1)}, u32[]{:S(2)}, u32[]{:S(2)}) collective-permute-start(bf16[128,1,256]{2,0,1:T(8,128)(2,1)S(1)} %get-tuple-element.48), channel_id=1, source_target_pairs={{0,2},{2,4},{4,6},{6,8},{8,10},{10,12},{12,14},{14,16},{16,18},{18... | collective-permute-start | bytes 196616 | tf_op jit(solution)/shard_map/ppermute | solution.py:19
  127.2 4.2 %collective-permute-start.9 = (bf16[128,1,256]{2,0,1:T(8,128)(2,1)S(1)}, bf16[128,1,256]{2,0,1:T(8,128)(2,1)S(1)}, u32[]{:S(2)}, u32[]{:S(2)}) collective-permute-start(bf16[128,1,256]{2,0,1:T(8,128)(2,1)S(1)} %get-tuple-element.49), channel_id=1, source_target_pairs={{2,0},{4,2},{6,4},{8,6},{10,8},{12,10},{14,12},{16,14},{18,16},{20... | collective-permute-start | bytes 196616 | tf_op jit(solution)/shard_map/ppermute | solution.py:21
  136.8 7.3 %collective-permute-start.10 = (bf16[128,1,256]{2,0,1:T(8,128)(2,1)S(1)}, bf16[128,1,256]{2,0,1:T(8,128)(2,1)S(1)}, u32[]{:S(2)}, u32[]{:S(2)}) collective-permute-start(bf16[128,1,256]{2,0,1:T(8,128)(2,1)S(1)} %get-tuple-element.46), channel_id=1, source_target_pairs={{0,2},{2,4},{4,6},{6,8},{8,10},{10,12},{12,14},{14,16},{16,18},{18... | collective-permute-start | bytes 196616 | tf_op jit(solution)/shard_map/ppermute | solution.py:19
  140.2 4.0 %collective-permute-start.11 = (bf16[128,1,256]{2,0,1:T(8,128)(2,1)S(1)}, bf16[128,1,256]{2,0,1:T(8,128)(2,1)S(1)}, u32[]{:S(2)}, u32[]{:S(2)}) collective-permute-start(bf16[128,1,256]{2,0,1:T(8,128)(2,1)S(1)} %get-tuple-element.47), channel_id=1, source_target_pairs={{2,0},{4,2},{6,4},{8,6},{10,8},{12,10},{14,12},{16,14},{18,16},{20... | collective-permute-start | bytes 196616 | tf_op jit(solution)/shard_map/ppermute | solution.py:21
  149.9 10.7 %collective-permute-start.12 = (bf16[128,1,256]{2,0,1:T(8,128)(2,1)S(1)}, bf16[128,1,256]{2,0,1:T(8,128)(2,1)S(1)}, u32[]{:S(2)}, u32[]{:S(2)}) collective-permute-start(bf16[128,1,256]{2,0,1:T(8,128)(2,1)S(1)} %get-tuple-element.44), channel_id=1, source_target_pairs={{0,2},{2,4},{4,6},{6,8},{8,10},{10,12},{12,14},{14,16},{16,18},{18... | collective-permute-start | bytes 196616 | tf_op jit(solution)/shard_map/ppermute | solution.py:19
  154.3 6.2 %collective-permute-start.13 = (bf16[128,1,256]{2,0,1:T(8,128)(2,1)S(1)}, bf16[128,1,256]{2,0,1:T(8,128)(2,1)S(1)}, u32[]{:S(2)}, u32[]{:S(2)}) collective-permute-start(bf16[128,1,256]{2,0,1:T(8,128)(2,1)S(1)} %get-tuple-element.45), channel_id=1, source_target_pairs={{2,0},{4,2},{6,4},{8,6},{10,8},{12,10},{14,12},{16,14},{18,16},{20... | collective-permute-start | bytes 196616 | tf_op jit(solution)/shard_map/ppermute | solution.py:21
  (20 other events, 23.6 us)
Sparse Core Ops, SparseCore 0:
  160.7 126.6 all-reduce.8
where the time goes:
time: 297 us; the launch traced here: 296 us
  blocking collectives  111 us (37%)
  waiting for transfers between devices  83.2 us (28%)
  starting transfers between devices  32 us (11%)
  matrix products  27.1 us (9%)
  local copies, waits for them, and re-layouts  16 us (5%)
  between operations  15 us (5%)
  other arithmetic  11 us (4%)
    unnamed x2, waiting for transfers between devices  80.1 us
    all_gather x1, blocking collectives, per_device(): lax.all_gather(gate_weights, ('rows', 'maze'), axis=0, tiled=True)  71.2 us
    psum x1, blocking collectives, per_device(): grad_table = lax.psum(pieces, ('rows', 'maze')) * scale  40 us
    ppermute x7, starting transfers between devices, extended(): lax.ppermute(tail, axis, [(i, (i + 1) % count) for i in range(ends)])  22.6 us
    unnamed x63, local copies, waits for them, and re-layouts  9.98 us
    dot_general x27, matrix products, gate_conv(): jnp.einsum('gc,crq->grq', kernel[tap_index], window, preferred_element_ty...  9.61 us
    ppermute x7, starting transfers between devices, extended(): lax.ppermute(head, axis, [((i + 1) % count, i) for i in range(ends)])  9.43 us
    dot_general x27, matrix products, weight_grads(): jnp.einsum('grq,crq->gc', gate_grad, window, preferred_element_type=jnp.f...  8.86 us
  transfers between devices with their start and end apart: 15, of which 3 were waited for; matrix products, arithmetic and copies ran while one was open for 7% of the time, Pallas kernels for 0%

commit v1 on v0

v1 whole, which is shorter than its diff:
```python
import functools
import math

import jax
import jax.numpy as jnp
from jax import lax
from jax.experimental import pallas as pl
from jax.experimental.pallas import tpu as pltpu
from jax.sharding import PartitionSpec as P

goal_reach = 64.0
MESH = pl.DeviceIdType.MESH
VMEM = pl.BlockSpec(memory_space=pltpu.VMEM)
SMEM = pl.BlockSpec(memory_space=pltpu.SMEM)
direct_limit = 64


def flat_peer(index, mazes):
    return {"rows": lax.div(index, mazes), "maze": lax.rem(index, mazes)}


def flat_self(mazes):
    return lax.axis_index("rows") * mazes + lax.axis_index("maze")


def greet_all(count, mazes):
    me = flat_self(mazes)
    barrier = pltpu.get_barrier_semaphore()

    def greet(step, _):
        peer = lax.rem(me + step, count)
        pl.semaphore_signal(
            barrier, inc=1, device_id=flat_peer(peer, mazes), device_id_type=MESH
        )
        return 0

    lax.fori_loop(1, count, greet, 0)
    pl.semaphore_wait(barrier, count - 1)


def gather_kernel(count, mazes, shard_ref, out_ref, send_sem, recv_sem):
    me = flat_self(mazes)
    greet_all(count, mazes)

    def push(step):
        return pltpu.make_async_remote_copy(
            src_ref=shard_ref,
            dst_ref=out_ref.at[me],
            send_sem=send_sem.at[step],
            recv_sem=recv_sem.at[step],
            device_id=flat_peer(lax.rem(me + step, count), mazes),
            device_id_type=MESH,
        )

    def start(step, _):
        push(step).start()
        return 0

    def finish(step, _):
        push(step).wait()
        return 0

    lax.fori_loop(1, count, start, 0)
    out_ref[me] = shard_ref[...]
    lax.fori_loop(1, count, finish, 0)


def gather_weights(shard, count, mazes):
    size = shard.shape[0]
    if size % 128 or count > direct_limit:
        return lax.all_gather(shard, ("rows", "maze"), axis=0, tiled=True)
    height = size // 128
    out = pl.pallas_call(
        functools.partial(gather_kernel, count, mazes),
        out_shape=jax.ShapeDtypeStruct((count, height, 128), shard.dtype),
        in_specs=[VMEM],
        out_specs=VMEM,
        scratch_shapes=[
            pltpu.SemaphoreType.DMA((count,)),
            pltpu.SemaphoreType.DMA((count,)),
        ],
        compiler_params=pltpu.CompilerParams(collective_id=0, has_side_effects=True),
    )(shard.reshape(height, 128))
    return out.reshape(-1)


def scatter_kernel(
    count, mazes, height, scale, chunk_ref, weight_ref, table_ref, landed, send_sem, recv_sem
):
    me = flat_self(mazes)
    greet_all(count, mazes)

    def push(step):
        peer = lax.rem(me + step, count)
        return pltpu.make_async_remote_copy(
            src_ref=chunk_ref.at[peer],
            dst_ref=landed.at[me],
            send_sem=send_sem.at[step],
            recv_sem=recv_sem.at[step],
            device_id=flat_peer(peer, mazes),
            device_id_type=MESH,
        )

    def start(step, _):
        push(step).start()
        return 0

    def finish(step, _):
        push(step).wait()
        return 0

    lax.fori_loop(1, count, start, 0)
    landed[me] = chunk_ref[me]
    lax.fori_loop(1, count, finish, 0)
    total = landed[0]
    for slot in range(1, count):
        total = total + landed[slot]
    total = total * scale
    weight_ref[...] = total[:height]
    table_ref[...] = total[height : height + 3, : table_ref.shape[1]]


def scatter_grads(chunks, height, input_width, scale, count, mazes):
    return pl.pallas_call(
        functools.partial(scatter_kernel, count, mazes, height, scale),
        out_shape=(
            jax.ShapeDtypeStruct((height, 128), jnp.float32),
            jax.ShapeDtypeStruct((3, input_width), jnp.float32),
        ),
        in_specs=[VMEM],
        out_specs=(VMEM, VMEM),
        scratch_shapes=[
            pltpu.VMEM(chunks.shape, jnp.float32),
            pltpu.SemaphoreType.DMA((count,)),
            pltpu.SemaphoreType.DMA((count,)),
        ],
        compiler_params=pltpu.CompilerParams(collective_id=2, has_side_effects=True),
    )(chunks)


def logistic(x):
    return 0.5 * jnp.tanh(0.5 * x) + 0.5


def main_kernel(
    chunk_rows,
    goal_ref,
    walls_ref,
    embed_ref,
    hidden_ref,
    cell_ref,
    cot_ref,
    forward_ref,
    backward_ref,
    kernel_ref,
    table_ref,
    carry_h_ref,
    carry_c_ref,
    fields,
    grads,
    cells,
    acts,
    squashes,
    input_acc,
    kernel_acc,
    field_land,
    grad_land,
    field_send,
    field_recv,
    grad_send,
    grad_recv,
):
    row_count, width, col_count = hidden_ref.shape
    in_width = embed_ref.shape[0]
    channels = in_width + width
    gates = 4 * width
    steps = cot_ref.shape[0]
    me = lax.axis_index("rows")
    ends = lax.axis_size("rows") - 1
    lane = lax.broadcasted_iota(jnp.int32, (1, col_count), 1)
    has_left = (lane > 0).astype(jnp.float32)
    has_right = (lane < col_count - 1).astype(jnp.float32)

    barrier = pltpu.get_barrier_semaphore()

    @pl.when(me > 0)
    def _():
        pl.semaphore_signal(barrier, inc=1, device_id={"rows": me - 1}, device_id_type=MESH)

    @pl.when(me < ends)
    def _():
        pl.semaphore_signal(barrier, inc=1, device_id={"rows": me + 1}, device_id_type=MESH)

    def masks(row):
        wall = (walls_ref[pl.ds(row, 1), :] == 1).astype(jnp.float32)
        row_dist = jnp.abs(me * row_count + row - goal_ref[0, 0])
        dist = (row_dist + jnp.abs(lane - goal_ref[0, 1])).astype(jnp.float32)
        return 1.0 - wall, wall, jnp.exp(-dist / goal_reach)

    def set_field(step, row, low, values):
        high = low + values.shape[0]
        wide = values.astype(jnp.float32)
        fields[step, row, low:high] = (pltpu.roll(wide, 1, 1) * has_left).astype(jnp.bfloat16)
        fields[step, row, channels + low : channels + high] = values
        fields[step, row, 2 * channels + low : 2 * channels + high] = (
            pltpu.roll(wide, col_count - 1, 1) * has_right
        ).astype(jnp.bfloat16)

    def share_inputs(step, row):
        for tap in range(3):
            part = slice(tap * channels, tap * channels + in_width)
            fields[step, row, part] = fields[0, row, part]

    def first_row(row, _):
        open_mask, wall_mask, bump = masks(row)
        values = (
            embed_ref[:, 0:1] * open_mask + embed_ref[:, 1:2] * wall_mask + embed_ref[:, 2:3] * bump
        ).astype(jnp.bfloat16)
        set_field(0, row + 1, 0, values)
        set_field(0, row + 1, in_width, hidden_ref[row])
        for step in range(1, steps):
            share_inputs(step, row + 1)
        cells[0, row] = cell_ref[row]
        return 0

    lax.fori_loop(0, row_count, first_row, 0)

    middle = jnp.logical_and(me > 0, me < ends)

    @pl.when(middle)
    def _():
        pl.semaphore_wait(barrier, 2)

    @pl.when(jnp.logical_not(middle))
    def _():
        pl.semaphore_wait(barrier, 1)

    def field_copy(step, side):
        low = channels if step == 0 else channels + in_width
        size = 2 * channels - low
        row = 1 if side == 0 else row_count
        return pltpu.make_async_remote_copy(
            src_ref=fields.at[step, row, pl.ds(low, size)],
            dst_ref=field_land.at[step, 1 - side, pl.ds(low - channels, size)],
            send_sem=field_send.at[step, side],
            recv_sem=field_recv.at[step, 1 - side],
            device_id={"rows": me - 1 if side == 0 else me + 1},
            device_id_type=MESH,
        )

    def grad_copy(step, side):
        row = 1 if side == 0 else row_count
        return pltpu.make_async_remote_copy(
            src_ref=grads.at[step, row],
            dst_ref=grad_land.at[step, 1 - side],
            send_sem=grad_send.at[step, side],
            recv_sem=grad_recv.at[step, 1 - side],
            device_id={"rows": me - 1 if side == 0 else me + 1},
            device_id_type=MESH,
        )

    def send_both(copy, step):
        @pl.when(me > 0)
        def _():
            copy(step, 0).start()

        @pl.when(me < ends)
        def _():
            copy(step, 1).start()

    def take_fields(step):
        low = 0 if step == 0 else in_width
        for side, row, there in ((0, 0, me > 0), (1, row_count + 1, me < ends)):

            @pl.when(there)
            def _():
                field_copy(step, side).wait_send()
                field_copy(step, 1 - side).wait_recv()
                if step:
                    share_inputs(step, row)
                set_field(step, row, low, field_land[step, side, low:channels])

            @pl.when(jnp.logical_not(there))
            def _():
                fields[step, row] = jnp.zeros((3 * channels, col_count), jnp.bfloat16)

    def take_grads(step):
        for side, row, there in ((0, 0, me > 0), (1, row_count + 1, me < ends)):

            @pl.when(there)
            def _():
                grad_copy(step, side).wait_send()
                grad_copy(step, 1 - side).wait_recv()
                grads[step, row] = grad_land[step, side]

            @pl.when(jnp.logical_not(there))
            def _():
                grads[step, row] = jnp.zeros((gates, col_count), jnp.bfloat16)

    def window(step, row):
        return fields[step, pl.ds(row, 3)].reshape(9 * channels, col_count)

    def forward_row(step, row):
        pre = jnp.dot(forward_ref[...], window(step, row), preferred_element_type=jnp.float32)
        in_gate = logistic(pre[:width])
        forget_gate = logistic(pre[width : 2 * width] + 1.0)
        out_gate = logistic(pre[2 * width : 3 * width])
        cand = jnp.tanh(pre[3 * width :])
        new_cell = forget_gate * cells[step, row] + in_gate * cand
        squash = jnp.tanh(new_cell)
        acts[step, row, :width] = in_gate
        acts[step, row, width : 2 * width] = forget_gate
        acts[step, row, 2 * width : 3 * width] = out_gate
        acts[step, row, 3 * width :] = cand
        squashes[step, row] = squash
        if step < steps - 1:
            cells[step + 1, row] = new_cell
            set_field(step + 1, row + 1, in_width, (out_gate * squash).astype(jnp.bfloat16))

    def for_rows(low, high, body):
        def run(row, _):
            body(row)
            return 0

        lax.fori_loop(low, high, run, 0)

    for step in range(steps):
        send_both(field_copy, step)
        for_rows(1, row_count - 1, functools.partial(forward_row, step))
        take_fields(step)
        forward_row(step, 0)
        forward_row(step, row_count - 1)

    def gate_row(step, row):
        in_gate = acts[step, row, :width]
        forget_gate = acts[step, row, width : 2 * width]
        out_gate = acts[step, row, 2 * width : 3 * width]
        cand = acts[step, row, 3 * width :]
        squash = squashes[step, row]
        hid_grad = cot_ref[step, row].astype(jnp.float32)
        if step < steps - 1:
            hid_grad = hid_grad + carry_h_ref[row]
        cell_grad = hid_grad * out_gate * (1.0 - squash * squash)
        if step < steps - 1:
            cell_grad = cell_grad + carry_c_ref[row]
        parts = (
            cell_grad * cand * in_gate * (1.0 - in_gate),
            cell_grad * cells[step, row] * forget_gate * (1.0 - forget_gate),
            hid_grad * squash * out_gate * (1.0 - out_gate),
            cell_grad * in_gate * (1.0 - cand * cand),
        )
        for index, part in enumerate(parts):
            grads[step, row + 1, index * width : (index + 1) * width] = part.astype(jnp.bfloat16)
        carry_c_ref[row] = cell_grad * forget_gate

    def back_row(step, row):
        stack = grads[step, pl.ds(row, 3)].reshape(3 * gates, col_count)
        out = jnp.dot(backward_ref[...], stack, preferred_element_type=jnp.float32)
        summed = (
            pltpu.roll(out[:channels], col_count - 1, 1) * has_right
            + out[channels : 2 * channels]
            + pltpu.roll(out[2 * channels :], 1, 1) * has_left
        )
        if step < steps - 1:
            input_acc[row] = input_acc[row] + summed[:in_width]
        else:
            input_acc[row] = summed[:in_width]
        carry_h_ref[row] = summed[in_width:]

    def kernel_rows(step, row):
        total = None
        for part in range(2):
            term = lax.dot_general(
                grads[step, row + part + 1],
                window(step, row + part),
                (((1,), (1,)), ((), ())),
                preferred_element_type=jnp.float32,
            )
            total = term if total is None else total + term
        for block in range(kernel_acc.shape[0]):
            part = total[:, block * 128 : (block + 1) * 128]
            lanes = part.shape[1]
            kernel_acc[block, :, :lanes] = kernel_acc[block, :, :lanes] + part

    kernel_acc[...] = jnp.zeros(kernel_acc.shape, jnp.float32)
    for step in reversed(range(steps)):
        gate_row(step, 0)
        gate_row(step, row_count - 1)
        send_both(grad_copy, step)
        for_rows(1, row_count - 1, functools.partial(gate_row, step))
        for_rows(1, row_count - 1, functools.partial(back_row, step))
        for_rows(0, row_count // 2, lambda pair: kernel_rows(step, 2 * pair))
        take_grads(step)
        back_row(step, 0)
        back_row(step, row_count - 1)

    def table_row(row, sums):
        grad = input_acc[row]
        return tuple(total + grad * mask for total, mask in zip(sums, masks(row)))

    zero = jnp.zeros((in_width, col_count), jnp.float32)
    sums = lax.fori_loop(0, row_count, table_row, (zero, zero, zero))
    columns = lax.broadcasted_iota(jnp.int32, (128, 128), 1)
    table = jnp.zeros((128, 128), jnp.float32)
    for index, total in enumerate(sums):
        column = jnp.sum(total, axis=1, keepdims=True)
        column = jnp.concatenate([column, jnp.zeros((128 - in_width, 1), jnp.float32)], axis=0)
        table = jnp.where(columns == index, column, table)
    flipped = table.T

    if chunk_rows:
        half = columns[: gates // 2] < channels
        lines = []
        for pair in range(5):
            even = kernel_acc[pair, pl.ds(0, gates // 2, stride=2), :]
            odd = kernel_acc[pair, pl.ds(1, gates // 2, stride=2), :]
            lines.append(jnp.where(half, even, pltpu.roll(odd, 64, 1)))
            if pair < 4:
                lines.append(jnp.where(half, pltpu.roll(even, 64, 1), odd))
        flat = jnp.concatenate(lines, axis=0)
        for index in range(kernel_ref.shape[0]):
            kernel_ref[index, :chunk_rows] = flat[index * chunk_rows : (index + 1) * chunk_rows]
            kernel_ref[index, chunk_rows : chunk_rows + 3] = flipped[:3]
            rest = kernel_ref.shape[1] - chunk_rows - 3
            kernel_ref[index, chunk_rows + 3 :] = jnp.zeros((rest, 128), jnp.float32)
    else:
        for block in range(kernel_acc.shape[0]):
            lanes = min(128, 9 * channels - block * 128)
            kernel_ref[:, block * 128 : block * 128 + lanes] = kernel_acc[block, :, :lanes]
    table_ref[...] = flipped[:8]


def per_device(
    maze_walls, goal_cell, start_hidden, start_cell, cotangent, gate_weights, embed_table
):
    rows = lax.axis_size("rows")
    mazes = lax.axis_size("maze")
    count = rows * mazes
    row_count = maze_walls.shape[1]
    col_count = maze_walls.shape[2]
    width = start_hidden.shape[1]
    in_width = embed_table.shape[1]
    channels = in_width + width
    gates = 4 * width
    steps = cotangent.shape[1]
    size = gate_weights.shape[0]
    kernel = gather_weights(gate_weights, count, mazes).reshape(3, 3, gates, channels)
    forward = kernel.transpose(2, 0, 1, 3).reshape(gates, 9 * channels)
    backward = kernel[::-1].transpose(1, 3, 0, 2).reshape(3 * channels, 3 * gates)
    hidden = start_hidden[0].transpose(1, 0, 2)
    cell = start_cell[0].transpose(1, 0, 2)
    cot = cotangent[0].transpose(0, 2, 1, 3)
    scale = 1.0 / math.sqrt(count * row_count * col_count * steps)

    direct = size % 128 == 0 and count <= direct_limit and channels == 64
    chunk_rows = size // 128 if direct else 0
    if direct:
        kernel_shape = (count, -(-(chunk_rows + 3) // 8) * 8, 128)
    else:
        kernel_shape = (gates, 9 * channels)
    f32 = jnp.float32
    bf16 = jnp.bfloat16
    grad_kernel, table, carry_h, carry_c = pl.pallas_call(
        functools.partial(main_kernel, chunk_rows),
        out_shape=(
            jax.ShapeDtypeStruct(kernel_shape, f32),
            jax.ShapeDtypeStruct((8, 128), f32),
            jax.ShapeDtypeStruct((row_count, width, col_count), f32),
            jax.ShapeDtypeStruct((row_count, width, col_count), f32),
        ),
        in_specs=[SMEM] + [VMEM] * 7,
        out_specs=(VMEM, VMEM, VMEM, VMEM),
        scratch_shapes=[
            pltpu.VMEM((steps, row_count + 2, 3 * channels, col_count), bf16),
            pltpu.VMEM((steps, row_count + 2, gates, col_count), bf16),
            pltpu.VMEM((steps, row_count, width, col_count), f32),
            pltpu.VMEM((steps, row_count, gates, col_count), f32),
            pltpu.VMEM((steps, row_count, width, col_count), f32),
            pltpu.VMEM((row_count, in_width, col_count), f32),
            pltpu.VMEM((-(-9 * channels // 128), gates, 128), f32),
            pltpu.VMEM((steps, 2, channels, col_count), bf16),
            pltpu.VMEM((steps, 2, gates, col_count), bf16),
            pltpu.SemaphoreType.DMA((steps, 2)),
            pltpu.SemaphoreType.DMA((steps, 2)),
            pltpu.SemaphoreType.DMA((steps, 2)),
            pltpu.SemaphoreType.DMA((steps, 2)),
        ],
        compiler_params=pltpu.CompilerParams(
            collective_id=1, has_side_effects=True, vmem_limit_bytes=48 * 1024 * 1024
        ),
    )(
        goal_cell,
        maze_walls[0],
        embed_table.T,
        hidden,
        cell,
        cot,
        forward,
        backward,
    )
    if direct:
        grad_weights, grad_table = scatter_grads(
            grad_kernel, chunk_rows, in_width, scale, count, mazes
        )
        grad_weights = grad_weights.reshape(-1)
    else:
        ordered = grad_kernel.reshape(gates, 9, channels).transpose(1, 0, 2).reshape(-1)
        grad_weights = scale * lax.psum_scatter(
            ordered, ("rows", "maze"), scatter_dimension=0, tiled=True
        )
        grad_table = scale * lax.psum(table[:3, :in_width], ("rows", "maze"))
    return (
        grad_weights,
        grad_table,
        carry_h.transpose(1, 0, 2)[None],
        carry_c.transpose(1, 0, 2)[None],
    )


def solution(mesh):
    return jax.shard_map(
        per_device,
        mesh=mesh,
        in_specs=(
            P("maze", "rows", None),
            P("maze", None),
            P("maze", None, "rows", None),
            P("maze", None, "rows", None),
            P("maze", None, None, "rows", None),
            P(("rows", "maze")),
            P(),
        ),
        out_specs=(
            P(("rows", "maze")),
            P(),
            P("maze", None, "rows", None),
            P("maze", None, "rows", None),
        ),
        check_vma=False,
    )
```

time: 297 us -> 62.2 us (0.21)
  blocking collectives: 111 us -> 0 us
  waiting for transfers between devices: 83.2 us -> 0 us
  Pallas kernels: 0 us -> 51.1 us
  starting transfers between devices: 32 us -> 0 us
  matrix products: 27.1 us -> 0 us
  between operations: 15 us -> 0.74 us
  other arithmetic: 11 us -> 0 us
  local copies, waits for them, and re-layouts: 16 us -> 9.45 us
    unnamed x2 -> x0, waiting for transfers between devices: 80.1 us -> none
    all_gather x1 -> x0, blocking collectives: 71.2 us -> none  [per_device(): lax.all_gather(gate_weights, ('rows', 'maze'), axis=0, tiled=True)]
    pallas_call x0 -> x3, Pallas kernels: none -> 51.1 us  [the longest x1 22 us: per_device(): pl.pallas_call(functools.partial(main_kernel, chunk_rows), out_shape=(jax...]
    psum x1 -> x0, blocking collectives: 40 us -> none  [per_device(): grad_table = lax.psum(pieces, ('rows', 'maze')) * scale]
    ppermute x14 -> x0, starting transfers between devices: 32 us -> none  [the longest x7 22.6 us: extended(): lax.ppermute(tail, axis, [(i, (i + 1) % count) for i in range(ends)])]
    dot_general x81 -> x0, matrix products: 27.1 us -> none  [the longest x27 9.61 us: gate_conv(): jnp.einsum('gc,crq->grq', kernel[tap_index], window, preferred_element_ty...]
    slice x16 -> x0, local copies, waits for them, and re-layouts: 4.17 us -> none  [the longest x4 1.36 us: extended(): lax.slice_in_dim(cells, cells.shape[dim] - width, cells.shape[dim], axis=...]
    ppermute x14 -> x0, waiting for transfers between devices: 3.16 us -> none  [the longest x7 3.14 us: extended(): lax.ppermute(head, axis, [((i + 1) % count, i) for i in range(ends)])]
  transfers between devices with their start and end apart: 15 -> 0, of which waited for: 3 -> 0; matrix products, arithmetic and copies ran while one was open for 7% -> 0% of each run, Pallas kernels for 0% -> 0%
where the time goes in v1:
time: 62.2 us; the launch traced here: 61.3 us
  Pallas kernels  51.1 us (82%)
  local copies, waits for them, and re-layouts  9.45 us (15%)
  between operations  0.74 us (1%)
    pallas_call x1, Pallas kernels, per_device(): pl.pallas_call(functools.partial(main_kernel, chunk_rows), out_shape=(jax...  22 us
    pallas_call x1, Pallas kernels, scatter_grads(): pl.pallas_call(functools.partial(scatter_kernel, count, mazes, height, sc...  16.4 us
    pallas_call x1, Pallas kernels, gather_weights(): pl.pallas_call(functools.partial(gather_kernel, count, mazes), out_shape=...  12.8 us
    unnamed x25, local copies, waits for them, and re-layouts  7.76 us

profile of v1, /device:TPU:0, one launch (start us, length us, event | category | flops | bytes accessed | tf_op | source)
XLA Modules:
  0.0 61.3 jit_solution(14175305955710907181)
XLA Ops:
  0.6 0.7 %copy-done.6 = f32[3,32]{1,0:T(4,128)S(1)} copy-done((f32[3,32]{1,0:T(4,128)S(1)}, f32[3,32]{1,0:T(4,128)}, u32[]{:S(2)}) %copy-start.6) | copy-done | bytes 408
  1.3 0.1 copy.19
  1.4 0.9 %copy.36 = bf16[1,32,8,256]{3,1,2,0:T(8,128)(2,1)S(1)} copy(bf16[1,32,8,256]{3,2,1,0:T(8,128)(2,1)} %param.9) | data formatting | bytes 262144 | tf_op args[2]
  2.3 12.8 %shard_map.102 = bf16[32,18,128]{2,1,0:T(8,128)(2,1)} custom-call(bf16[18,128]{1,0:T(8,128)(2,1)} %bitcast.46), custom_call_target="tpu_custom_call" | custom-call | tf_op jit(solution)/shard_map/pallas_call | solution.py:73
  15.1 1.1 %reshape_reshape.3 = bf16[3,3,128,64]{3,2,1,0:T(8,128)(2,1)S(1)} reshape(bf16[32,18,128]{2,1,0:T(8,128)(2,1)} %shard_map.102) | data formatting | bytes 294912 | tf_op jit(solution)/shard_map/reshape;reshape | solution.py:447
  16.2 0.2 copy.23
  16.4 0.2 copy.25.forward_ref
  16.6 0.8 %copy-done.4 = f32[1,32,8,256]{3,2,1,0:T(8,128)S(1)} copy-done((f32[1,32,8,256]{3,2,1,0:T(8,128)S(1)}, f32[1,32,8,256]{3,2,1,0:T(8,128)}, u32[]{:S(2)}) %copy-start.4) | copy-done | bytes 262168
  17.4 0.1 copy.34
  17.5 0.0 copy-start.3
  17.5 0.2 copy.24
  17.7 0.8 %copy-done.3 = bf16[1,3,32,8,256]{4,3,2,1,0:T(8,128)(2,1)S(1)} copy-done((bf16[1,3,32,8,256]{4,3,2,1,0:T(8,128)(2,1)S(1)}, bf16[1,3,32,8,256]{4,3,2,1,0:T(8,128)(2,1)}, u32[]{:S(2)}) %copy-start.3) | copy-done | bytes 393240
  18.5 0.1 copy.33
  18.6 0.0 copy-start.2
  18.6 0.6 copy-done.1
  19.2 0.1 copy-done.2
  19.2 22.0 %shard_map.103 = (f32[32,24,128]{2,1,0:T(8,128)S(1)}, f32[8,128]{1,0:T(8,128)}, f32[8,32,256]{2,1,0:T(8,128)S(1)}, f32[8,32,256]{2,1,0:T(8,128)S(1)}) custom-call(s32[1,2]{1,0:T(1,128)S(1)} %copy-done.2, s32[8,256]{1,0:T(8,128)S(1)} %bitcast.41, f32[32,3]{1,0:T(8,128)S(1)} %bitcast.40, bf16[8,32,256]{2,1,0:T(8,128)(2,1)S(1)} %bitcast.37, ...), custom_call_target="tpu_custom_call" | custom-call | tf_op jit(solution)/shard_map/pallas_call | solution.py:463
  41.2 0.7 %copy-done = f32[32,24,128]{2,1,0:T(8,128)} copy-done((f32[32,24,128]{2,1,0:T(8,128)}, f32[32,24,128]{2,1,0:T(8,128)S(1)}, u32[]{:S(2)}) %copy-start) | copy-done | bytes 393240
  42.0 16.4 %shard_map.104 = (f32[18,128]{1,0:T(8,128)}, f32[3,32]{1,0:T(4,128)}) custom-call(f32[32,24,128]{2,1,0:T(8,128)} %copy-done), custom_call_target="tpu_custom_call" | custom-call | tf_op jit(solution)/shard_map/pallas_call | solution.py:124
  58.3 0.9 %copy.26 = f32[1,32,8,256]{3,2,1,0:T(8,128)} copy(f32[1,32,8,256]{3,1,2,0:T(8,128)S(1)} %bitcast.39) | data formatting | bytes 524288
  59.2 0.9 %copy.27 = f32[1,32,8,256]{3,2,1,0:T(8,128)} copy(f32[1,32,8,256]{3,1,2,0:T(8,128)S(1)} %bitcast.38) | data formatting | bytes 524288
  60.0 0.6 copy.39
  60.6 0.1 copy-done.7
  60.7 0.6 copy.40
  (9 shorter events, 0.1 us)
Async XLA Ops:
  0.6 0.7 %copy-start.6 = (f32[3,32]{1,0:T(4,128)S(1)}, f32[3,32]{1,0:T(4,128)}, u32[]{:S(2)}) copy-start(f32[3,32]{1,0:T(4,128)} %param.13) | copy-start | bytes 1156
  16.4 1.0 %copy-start.4 = (f32[1,32,8,256]{3,2,1,0:T(8,128)S(1)}, f32[1,32,8,256]{3,2,1,0:T(8,128)}, u32[]{:S(2)}) copy-start(f32[1,32,8,256]{3,2,1,0:T(8,128)} %param.10) | copy-start | bytes 786436
  17.5 1.0 %copy-start.3 = (bf16[1,3,32,8,256]{4,3,2,1,0:T(8,128)(2,1)S(1)}, bf16[1,3,32,8,256]{4,3,2,1,0:T(8,128)(2,1)}, u32[]{:S(2)}) copy-start(bf16[1,3,32,8,256]{4,3,2,1,0:T(8,128)(2,1)} %param.11) | copy-start | bytes 1179652
  18.5 0.7 %copy-start.1 = (s32[1,8,256]{2,1,0:T(8,128)S(1)}, s32[1,8,256]{2,1,0:T(8,128)}, u32[]{:S(2)}) copy-start(s32[1,8,256]{2,1,0:T(8,128)} %param.7) | copy-start | bytes 24580
  18.6 0.7 %copy-start.2 = (s32[1,2]{1,0:T(1,128)S(1)}, s32[1,2]{1,0:T(1,128)}, u32[]{:S(2)}) copy-start(s32[1,2]{1,0:T(1,128)} %goal_ref.1) | copy-start | bytes 28
  41.2 0.7 %copy-start = (f32[32,24,128]{2,1,0:T(8,128)}, f32[32,24,128]{2,1,0:T(8,128)S(1)}, u32[]{:S(2)}) copy-start(f32[32,24,128]{2,1,0:T(8,128)S(1)} %get-tuple-element.9.chunk_ref) | copy-start | bytes 1179652
  59.2 0.9 %copy-start.5 = (f32[18,128]{1,0:T(8,128)S(1)}, f32[18,128]{1,0:T(8,128)}, u32[]{:S(2)}) copy-start(f32[18,128]{1,0:T(8,128)} %get-tuple-element.10) | copy-start | bytes 27652
  60.0 0.7 %copy-start.7 = (f32[3,32]{1,0:T(4,128)S(1)}, f32[3,32]{1,0:T(4,128)}, u32[]{:S(2)}) copy-start(f32[3,32]{1,0:T(4,128)} %get-tuple-element.27) | copy-start | bytes 1156

commit v2 on v1

--- a/solution.py
+++ b/solution.py
@@ -12,130 +12,57 @@
 MESH = pl.DeviceIdType.MESH
 VMEM = pl.BlockSpec(memory_space=pltpu.VMEM)
 SMEM = pl.BlockSpec(memory_space=pltpu.SMEM)
-direct_limit = 64
-
-
-def flat_peer(index, mazes):
-    return {"rows": lax.div(index, mazes), "maze": lax.rem(index, mazes)}
-
-
-def flat_self(mazes):
-    return lax.axis_index("rows") * mazes + lax.axis_index("maze")
-
-
-def greet_all(count, mazes):
-    me = flat_self(mazes)
-    barrier = pltpu.get_barrier_semaphore()
-
-    def greet(step, _):
-        peer = lax.rem(me + step, count)
-        pl.semaphore_signal(
-            barrier, inc=1, device_id=flat_peer(peer, mazes), device_id_type=MESH
-        )
-        return 0
-
-    lax.fori_loop(1, count, greet, 0)
-    pl.semaphore_wait(barrier, count - 1)
-
-
-def gather_kernel(count, mazes, shard_ref, out_ref, send_sem, recv_sem):
-    me = flat_self(mazes)
-    greet_all(count, mazes)
-
-    def push(step):
-        return pltpu.make_async_remote_copy(
-            src_ref=shard_ref,
-            dst_ref=out_ref.at[me],
-            send_sem=send_sem.at[step],
-            recv_sem=recv_sem.at[step],
-            device_id=flat_peer(lax.rem(me + step, count), mazes),
-            device_id_type=MESH,
-        )
-
-    def start(step, _):
-        push(step).start()
-        return 0
-
-    def finish(step, _):
-        push(step).wait()
-        return 0
-
-    lax.fori_loop(1, count, start, 0)
-    out_ref[me] = shard_ref[...]
-    lax.fori_loop(1, count, finish, 0)
-
-
-def gather_weights(shard, count, mazes):
-    size = shard.shape[0]
-    if size % 128 or count > direct_limit:
-        return lax.all_gather(shard, ("rows", "maze"), axis=0, tiled=True)
-    height = size // 128
-    out = pl.pallas_call(
-        functools.partial(gather_kernel, count, mazes),
-        out_shape=jax.ShapeDtypeStruct((count, height, 128), shard.dtype),
-        in_specs=[VMEM],
-        out_specs=VMEM,
-        scratch_shapes=[
-            pltpu.SemaphoreType.DMA((count,)),
-            pltpu.SemaphoreType.DMA((count,)),
-        ],
-        compiler_params=pltpu.CompilerParams(collective_id=0, has_side_effects=True),
-    )(shard.reshape(height, 128))
-    return out.reshape(-1)
-
-
-def scatter_kernel(
-    count, mazes, height, scale, chunk_ref, weight_ref, table_ref, landed, send_sem, recv_sem
-):
-    me = flat_self(mazes)
-    greet_all(count, mazes)
-
-    def push(step):
-        peer = lax.rem(me + step, count)
-        return pltpu.make_async_remote_copy(
-            src_ref=chunk_ref.at[peer],
-            dst_ref=landed.at[me],
-            send_sem=send_sem.at[step],
-            recv_sem=recv_sem.at[step],
-            device_id=flat_peer(peer, mazes),
-            device_id_type=MESH,
-        )
-
-    def start(step, _):
-        push(step).start()
-        return 0
-
-    def finish(step, _):
-        push(step).wait()
-        return 0
-
-    lax.fori_loop(1, count, start, 0)
-    landed[me] = chunk_ref[me]
-    lax.fori_loop(1, count, finish, 0)
-    total = landed[0]
-    for slot in range(1, count):
-        total = total + landed[slot]
-    total = total * scale
-    weight_ref[...] = total[:height]
-    table_ref[...] = total[height : height + 3, : table_ref.shape[1]]
-
-
-def scatter_grads(chunks, height, input_width, scale, count, mazes):
-    return pl.pallas_call(
-        functools.partial(scatter_kernel, count, mazes, height, scale),
-        out_shape=(
-            jax.ShapeDtypeStruct((height, 128), jnp.float32),
-            jax.ShapeDtypeStruct((3, input_width), jnp.float32),
-        ),
-        in_specs=[VMEM],
-        out_specs=(VMEM, VMEM),
-        scratch_shapes=[
-            pltpu.VMEM(chunks.shape, jnp.float32),
-            pltpu.SemaphoreType.DMA((count,)),
-            pltpu.SemaphoreType.DMA((count,)),
-        ],
-        compiler_params=pltpu.CompilerParams(collective_id=2, has_side_effects=True),
-    )(chunks)
+
+
+class Groups:
+    def __init__(self, depth):
+        rows = lax.axis_index("rows")
+        self.depth = depth
+        self.maze = lax.axis_index("maze")
+        self.core = lax.rem(rows, 2)
+        self.z = lax.div(rows, 4)
+        self.y = lax.rem(lax.div(rows, 2), 2)
+        self.plane = self.y * 2 + self.maze
+
+    def device(self, z, plane, core):
+        return {"rows": z * 4 + lax.div(plane, 2) * 2 + core, "maze": lax.rem(plane, 2)}
+
+    def z_peer(self, step):
+        z = lax.rem(self.z + step, self.depth)
+        return z, self.device(z, self.plane, self.core)
+
+    def plane_peer(self, step):
+        plane = lax.rem(self.plane + step, 4)
+        return plane, self.device(self.z, plane, self.core)
+
+    def core_peer(self):
+        return self.device(self.z, self.plane, 1 - self.core)
+
+    def peers(self):
+        found = [self.z_peer(step)[1] for step in range(1, self.depth)]
+        found += [self.plane_peer(step)[1] for step in range(1, 4)]
+        return found + [self.core_peer()]
+
+
+def shard_slots(depth):
+    return [
+        (core, 2 * y + maze, z)
+        for z in range(depth)
+        for y in range(2)
+        for core in range(2)
+        for maze in range(2)
+    ]
+
+
+def push(src, dst, sems, slot, device):
+    return pltpu.make_async_remote_copy(
+        src_ref=src,
+        dst_ref=dst,
+        send_sem=sems.at[0, slot],
+        recv_sem=sems.at[1, slot],
+        device_id=device,
+        device_id_type=MESH,
+    )
 
 
 def logistic(x):
@@ -143,19 +70,28 @@
 
 
 def main_kernel(
-    chunk_rows,
+    depth,
+    scale,
     goal_ref,
     walls_ref,
     embed_ref,
     hidden_ref,
     cell_ref,
     cot_ref,
-    forward_ref,
-    backward_ref,
-    kernel_ref,
-    table_ref,
-    carry_h_ref,
-    carry_c_ref,
+    *refs,
+):
+    if depth:
+        shard_ref, *refs = refs
+    else:
+        forward_ref, backward_ref, *refs = refs
+    kernel_ref, table_ref, carry_h_ref, carry_c_ref, *refs = refs
+    if depth:
+        refs, extra = refs[:-14], refs[-14:]
+        forward_ref, backward_ref, shards, chunks = extra[:4]
+        core_land, plane_land, z_sum, z_land = extra[4:8]
+        z_gather, plane_gather, core_gather = extra[8:11]
+        core_scatter, plane_scatter, z_scatter = extra[11:]
+    (
     fields,
     grads,
     cells,
@@ -169,7 +105,7 @@
     field_recv,
     grad_send,
     grad_recv,
-):
+    ) = refs
     row_count, width, col_count = hidden_ref.shape
     in_width = embed_ref.shape[0]
     channels = in_width + width
@@ -190,6 +126,37 @@
     @pl.when(me < ends)
     def _():
         pl.semaphore_signal(barrier, inc=1, device_id={"rows": me + 1}, device_id_type=MESH)
+
+    group_peers = 0
+    if depth:
+        groups = Groups(depth)
+        z_me, plane_me, core_me = groups.z, groups.plane, groups.core
+        for peer in groups.peers():
+            pl.semaphore_signal(barrier, inc=1, device_id=peer, device_id_type=MESH)
+            group_peers += 1
+        shards[core_me, plane_me, z_me] = shard_ref[...]
+    middle = jnp.logical_and(me > 0, me < ends)
+
+    @pl.when(middle)
+    def _():
+        pl.semaphore_wait(barrier, group_peers + 2)
+
+    @pl.when(jnp.logical_not(middle))
+    def _():
+        pl.semaphore_wait(barrier, group_peers + 1)
+
+    gathers = ([], [], [])
+    if depth:
+        for step in range(1, depth):
+            part = shards.at[core_me, plane_me, z_me]
+            gathers[0].append(push(part, part, z_gather, step, groups.z_peer(step)[1]))
+        for step in range(1, 4):
+            part = shards.at[core_me, plane_me]
+            gathers[1].append(push(part, part, plane_gather, step, groups.plane_peer(step)[1]))
+        part = shards.at[core_me]
+        gathers[2].append(push(part, part, core_gather, 0, groups.core_peer()))
+        for copy in gathers[0]:
+            copy.start()
 
     def masks(row):
         wall = (walls_ref[pl.ds(row, 1), :] == 1).astype(jnp.float32)
@@ -225,15 +192,6 @@
 
     lax.fori_loop(0, row_count, first_row, 0)
 
-    middle = jnp.logical_and(me > 0, me < ends)
-
-    @pl.when(middle)
-    def _():
-        pl.semaphore_wait(barrier, 2)
-
-    @pl.when(jnp.logical_not(middle))
-    def _():
-        pl.semaphore_wait(barrier, 1)
 
     def field_copy(step, side):
         low = channels if step == 0 else channels + in_width
@@ -324,8 +282,46 @@
 
         lax.fori_loop(low, high, run, 0)
 
+    def build_weights():
+        flat = jnp.concatenate(
+            [shards[slot].astype(jnp.float32) for slot in shard_slots(depth)], axis=0
+        )
+        size = gates // 2
+        half = lax.broadcasted_iota(jnp.int32, (size, 128), 1) < channels
+        for pair in range(5):
+            near = flat[2 * pair * size : (2 * pair + 1) * size]
+            far = flat[(2 * pair + 1) * size : (2 * pair + 2) * size] if pair < 4 else near
+            kernel_acc[pair, pl.ds(0, size, stride=2), :] = jnp.where(
+                half, near, pltpu.roll(far, 64, 1)
+            )
+            kernel_acc[pair, pl.ds(1, size, stride=2), :] = jnp.where(
+                half, pltpu.roll(near, 64, 1), far
+            )
+        for pair in range(5):
+            mixed = kernel_acc[pair]
+            flipped = mixed.T
+            for tap in range(2 * pair, min(2 * pair + 2, 9)):
+                low = (tap - 2 * pair) * channels
+                row_tap, col_tap = tap // 3, tap % 3
+                backward_ref[
+                    col_tap * channels : (col_tap + 1) * channels,
+                    (2 - row_tap) * gates : (3 - row_tap) * gates,
+                ] = flipped[low : low + channels].astype(jnp.bfloat16)
+            lanes = min(128, 9 * channels - pair * 128)
+            forward_ref[:, pair * 128 : pair * 128 + lanes] = mixed[:, :lanes].astype(jnp.bfloat16)
+
+    send_both(field_copy, 0)
+    if depth:
+        for stage in range(3):
+            for copy in gathers[stage]:
+                copy.wait()
+            if stage < 2:
+                for copy in gathers[stage + 1]:
+                    copy.start()
+        build_weights()
     for step in range(steps):
-        send_both(field_copy, step)
+        if step:
+            send_both(field_copy, step)
         for_rows(1, row_count - 1, functools.partial(forward_row, step))
         take_fields(step)
         forward_row(step, 0)
@@ -408,26 +404,60 @@
         table = jnp.where(columns == index, column, table)
     flipped = table.T
 
-    if chunk_rows:
-        half = columns[: gates // 2] < channels
-        lines = []
-        for pair in range(5):
-            even = kernel_acc[pair, pl.ds(0, gates // 2, stride=2), :]
-            odd = kernel_acc[pair, pl.ds(1, gates // 2, stride=2), :]
-            lines.append(jnp.where(half, even, pltpu.roll(odd, 64, 1)))
-            if pair < 4:
-                lines.append(jnp.where(half, pltpu.roll(even, 64, 1), odd))
-        flat = jnp.concatenate(lines, axis=0)
-        for index in range(kernel_ref.shape[0]):
-            kernel_ref[index, :chunk_rows] = flat[index * chunk_rows : (index + 1) * chunk_rows]
-            kernel_ref[index, chunk_rows : chunk_rows + 3] = flipped[:3]
-            rest = kernel_ref.shape[1] - chunk_rows - 3
-            kernel_ref[index, chunk_rows + 3 :] = jnp.zeros((rest, 128), jnp.float32)
-    else:
+    if not depth:
         for block in range(kernel_acc.shape[0]):
             lanes = min(128, 9 * channels - block * 128)
             kernel_ref[:, block * 128 : block * 128 + lanes] = kernel_acc[block, :, :lanes]
-    table_ref[...] = flipped[:8]
+        table_ref[...] = flipped[:3, :in_width]
+        return
+
+    chunk_rows = shard_ref.shape[0]
+    half = columns[: gates // 2] < channels
+    lines = []
+    for pair in range(5):
+        even = kernel_acc[pair, pl.ds(0, gates // 2, stride=2), :]
+        odd = kernel_acc[pair, pl.ds(1, gates // 2, stride=2), :]
+        lines.append(jnp.where(half, even, pltpu.roll(odd, 64, 1)))
+        if pair < 4:
+            lines.append(jnp.where(half, pltpu.roll(even, 64, 1), odd))
+    flat = jnp.concatenate(lines, axis=0)
+    rest = chunks.shape[3] - chunk_rows - 3
+    for index, slot in enumerate(shard_slots(depth)):
+        part = flat[index * chunk_rows : (index + 1) * chunk_rows]
+        pieces = [part, flipped[:3]]
+        if rest:
+            pieces.append(jnp.zeros((rest, 128), jnp.float32))
+        chunks[slot] = jnp.concatenate(pieces, axis=0)
+
+    copy = push(chunks.at[1 - core_me], core_land, core_scatter, 0, groups.core_peer())
+    copy.start()
+    copy.wait()
+    chunks[core_me] = chunks[core_me] + core_land[...]
+    copies = []
+    for step in range(1, 4):
+        plane, peer = groups.plane_peer(step)
+        copies.append(
+            push(chunks.at[core_me, plane], plane_land.at[plane_me], plane_scatter, step, peer)
+        )
+        copies[-1].start()
+    plane_land[plane_me] = chunks[core_me, plane_me]
+    for copy in copies:
+        copy.wait()
+    z_sum[...] = (plane_land[0] + plane_land[1]) + (plane_land[2] + plane_land[3])
+    copies = []
+    for step in range(1, depth):
+        z, peer = groups.z_peer(step)
+        copies.append(push(z_sum.at[z], z_land.at[z_me], z_scatter, step, peer))
+        copies[-1].start()
+    z_land[z_me] = z_sum[z_me]
+    for copy in copies:
+        copy.wait()
+    total = z_land[0]
+    for index in range(1, depth):
+        total = total + z_land[index]
+    total = total * scale
+    kernel_ref[...] = total[:chunk_rows]
+    table_ref[...] = total[chunk_rows : chunk_rows + 3, :in_width]
 
 
 def per_device(
@@ -444,31 +474,51 @@
     gates = 4 * width
     steps = cotangent.shape[1]
     size = gate_weights.shape[0]
-    kernel = gather_weights(gate_weights, count, mazes).reshape(3, 3, gates, channels)
-    forward = kernel.transpose(2, 0, 1, 3).reshape(gates, 9 * channels)
-    backward = kernel[::-1].transpose(1, 3, 0, 2).reshape(3 * channels, 3 * gates)
     hidden = start_hidden[0].transpose(1, 0, 2)
     cell = start_cell[0].transpose(1, 0, 2)
     cot = cotangent[0].transpose(0, 2, 1, 3)
     scale = 1.0 / math.sqrt(count * row_count * col_count * steps)
 
-    direct = size % 128 == 0 and count <= direct_limit and channels == 64
-    chunk_rows = size // 128 if direct else 0
+    direct = size % 128 == 0 and mazes == 2 and rows % 4 == 0 and channels == 64 and gates == 128
+    depth = rows // 4 if direct else 0
+    height = size // 128
     if direct:
-        kernel_shape = (count, -(-(chunk_rows + 3) // 8) * 8, 128)
+        weights = [gate_weights.reshape(height, 128)]
+        kernel_shape = (height, 128)
     else:
+        gathered = lax.all_gather(gate_weights, ("rows", "maze"), axis=0, tiled=True)
+        kernel = gathered.reshape(3, 3, gates, channels)
+        weights = [
+            kernel.transpose(2, 0, 1, 3).reshape(gates, 9 * channels),
+            kernel[::-1].transpose(1, 3, 0, 2).reshape(3 * channels, 3 * gates),
+        ]
         kernel_shape = (gates, 9 * channels)
     f32 = jnp.float32
     bf16 = jnp.bfloat16
+    direct_scratch = []
+    if direct:
+        tall = -(-(height + 3) // 8) * 8
+        direct_scratch = [
+            pltpu.VMEM((gates, 9 * channels), bf16),
+            pltpu.VMEM((3 * channels, 3 * gates), bf16),
+            pltpu.VMEM((2, 4, depth, height, 128), bf16),
+            pltpu.VMEM((2, 4, depth, tall, 128), f32),
+            pltpu.VMEM((4, depth, tall, 128), f32),
+            pltpu.VMEM((4, depth, tall, 128), f32),
+            pltpu.VMEM((depth, tall, 128), f32),
+            pltpu.VMEM((depth, tall, 128), f32),
+        ] + [
+            pltpu.SemaphoreType.DMA((2, slots)) for slots in (depth, 4, 1, 1, 4, depth)
+        ]
     grad_kernel, table, carry_h, carry_c = pl.pallas_call(
-        functools.partial(main_kernel, chunk_rows),
+        functools.partial(main_kernel, depth, scale),
         out_shape=(
             jax.ShapeDtypeStruct(kernel_shape, f32),
-            jax.ShapeDtypeStruct((8, 128), f32),
+            jax.ShapeDtypeStruct((3, in_width), f32),
             jax.ShapeDtypeStruct((row_count, width, col_count), f32),
             jax.ShapeDtypeStruct((row_count, width, col_count), f32),
         ),
-        in_specs=[SMEM] + [VMEM] * 7,
+        in_specs=[SMEM] + [VMEM] * (5 + len(weights)),
         out_specs=(VMEM, VMEM, VMEM, VMEM),
         scratch_shapes=[
             pltpu.VMEM((steps, row_count + 2, 3 * channels, col_count), bf16),
@@ -484,9 +534,10 @@
             pltpu.SemaphoreType.DMA((steps, 2)),
             pltpu.SemaphoreType.DMA((steps, 2)),
             pltpu.SemaphoreType.DMA((steps, 2)),
-        ],
+        ]
+        + direct_scratch,
         compiler_params=pltpu.CompilerParams(
-            collective_id=1, has_side_effects=True, vmem_limit_bytes=48 * 1024 * 1024
+            collective_id=0, has_side_effects=True, vmem_limit_bytes=48 * 1024 * 1024
         ),
     )(
         goal_cell,
@@ -495,20 +546,17 @@
         hidden,
         cell,
         cot,
-        forward,
-        backward,
+        *weights,
     )
     if direct:
-        grad_weights, grad_table = scatter_grads(
-            grad_kernel, chunk_rows, in_width, scale, count, mazes
-        )
-        grad_weights = grad_weights.reshape(-1)
+        grad_weights = grad_kernel.reshape(-1)
+        grad_table = table
     else:
         ordered = grad_kernel.reshape(gates, 9, channels).transpose(1, 0, 2).reshape(-1)
         grad_weights = scale * lax.psum_scatter(
             ordered, ("rows", "maze"), scatter_dimension=0, tiled=True
         )
-        grad_table = scale * lax.psum(table[:3, :in_width], ("rows", "maze"))
+        grad_table = scale * lax.psum(table, ("rows", "maze"))
     return (
         grad_weights,
         grad_table,

time: 62.2 us -> 50.8 us (0.82); the launches traced: 61.3 us -> 50.6 us
  Pallas kernels: 51.1 us -> 44.4 us
  local copies, waits for them, and re-layouts: 9.45 us -> 5.46 us
    pallas_call x3 -> x1, Pallas kernels: 51.1 us -> 44.4 us  [per_device(): pl.pallas_call(functools.partial(main_kernel, depth, scale), out_shape=(j...]
    unnamed x25 -> x20, local copies, waits for them, and re-layouts: 7.76 us -> 5.46 us
    another operation x1 -> x0, local copies, waits for them, and re-layouts: 1.14 us -> none  [per_device(): gather_weights(gate_weights, count, mazes).reshape(3, 3, gates, channels)]
where the time goes in v2:
time: 50.8 us; the launch traced here: 50.6 us
  Pallas kernels  44.4 us (87%)
  local copies, waits for them, and re-layouts  5.46 us (11%)
  between operations  0.72 us (1%)
    pallas_call x1, Pallas kernels, per_device(): pl.pallas_call(functools.partial(main_kernel, depth, scale), out_shape=(j...  44.4 us
    unnamed x20, local copies, waits for them, and re-layouts  5.46 us

profile of v2, /device:TPU:0, one launch (start us, length us, event | category | flops | bytes accessed | tf_op | source)
XLA Modules:
  0.0 50.6 jit_solution(12742935022141934944)
XLA Ops:
  0.6 0.0 copy-start.5
  0.6 0.0 copy-start.4
  0.7 0.7 %copy-done.5 = f32[3,32]{1,0:T(4,128)S(1)} copy-done((f32[3,32]{1,0:T(4,128)S(1)}, f32[3,32]{1,0:T(4,128)}, u32[]{:S(2)}) %copy-start.5) | copy-done | bytes 408
  1.3 0.1 copy.11
  1.4 0.0 copy-start.3
  1.4 1.0 %copy.22 = bf16[1,32,8,256]{3,1,2,0:T(8,128)(2,1)S(1)} copy(bf16[1,32,8,256]{3,2,1,0:T(8,128)(2,1)} %param.9) | data formatting | bytes 262144 | tf_op args[2]
  2.4 0.0 copy-done.4
  2.4 0.1 copy.21
  2.5 0.0 copy-done.3
  2.5 0.0 copy-start
  2.5 0.0 copy-start.1
  2.5 0.1 copy.20
  2.6 0.0 copy-start.2
  2.6 0.6 %copy-done = s32[1,8,256]{2,1,0:T(8,128)S(1)} copy-done((s32[1,8,256]{2,1,0:T(8,128)S(1)}, s32[1,8,256]{2,1,0:T(8,128)}, u32[]{:S(2)}) %copy-start) | copy-done | bytes 8216
  3.2 0.0 copy-done.1
  3.2 0.1 copy-done.2
  3.3 44.4 %shard_map.102 = (f32[18,128]{1,0:T(8,128)S(1)}, f32[3,32]{1,0:T(4,128)S(1)}, f32[8,32,256]{2,1,0:T(8,128)S(1)}, f32[8,32,256]{2,1,0:T(8,128)S(1)}) custom-call(s32[1,2]{1,0:T(1,128)S(1)} %copy-done.2, s32[8,256]{1,0:T(8,128)S(1)} %bitcast.32, f32[32,3]{1,0:T(8,128)S(1)} %bitcast.30, bf16[8,32,256]{2,1,0:T(8,128)(2,1)S(1)} %bitcast.27, ...), custom_call_target="tpu_custom_call" | custom-call | tf_op jit(solution)/shard_map/pallas_call | solution.py:513
  47.7 0.9 %copy.15 = f32[1,32,8,256]{3,2,1,0:T(8,128)} copy(f32[1,32,8,256]{3,1,2,0:T(8,128)S(1)} %bitcast.29) | data formatting | bytes 524288
  48.6 0.9 %copy.16 = f32[1,32,8,256]{3,2,1,0:T(8,128)} copy(f32[1,32,8,256]{3,1,2,0:T(8,128)S(1)} %bitcast.28) | data formatting | bytes 524288
  49.4 0.6 %copy.25 = f32[2304]{0:T(1024)} copy(f32[2304]{0:T(1024)S(1)} %bitcast.31) | data formatting | bytes 18432
  50.0 0.6 %copy.26 = f32[3,32]{1,0:T(4,128)} copy(f32[3,32]{1,0:T(4,128)S(1)} %get-tuple-element.21) | data formatting | bytes 768
Async XLA Ops:
  0.6 0.7 %copy-start.5 = (f32[3,32]{1,0:T(4,128)S(1)}, f32[3,32]{1,0:T(4,128)}, u32[]{:S(2)}) copy-start(f32[3,32]{1,0:T(4,128)} %param.13) | copy-start | bytes 1156
  0.6 1.7 %copy-start.4 = (f32[1,32,8,256]{3,2,1,0:T(8,128)S(1)}, f32[1,32,8,256]{3,2,1,0:T(8,128)}, u32[]{:S(2)}) copy-start(f32[1,32,8,256]{3,2,1,0:T(8,128)} %param.10) | copy-start | bytes 786436
  1.4 1.1 %copy-start.3 = (bf16[1,3,32,8,256]{4,3,2,1,0:T(8,128)(2,1)S(1)}, bf16[1,3,32,8,256]{4,3,2,1,0:T(8,128)(2,1)}, u32[]{:S(2)}) copy-start(bf16[1,3,32,8,256]{4,3,2,1,0:T(8,128)(2,1)} %param.11) | copy-start | bytes 1179652
  2.5 0.7 %copy-start = (s32[1,8,256]{2,1,0:T(8,128)S(1)}, s32[1,8,256]{2,1,0:T(8,128)}, u32[]{:S(2)}) copy-start(s32[1,8,256]{2,1,0:T(8,128)} %param.7) | copy-start | bytes 24580
  2.5 0.7 %copy-start.1 = (bf16[2304]{0:T(1024)(128)(2,1)S(1)}, bf16[2304]{0:T(1024)(128)(2,1)}, u32[]{:S(2)}) copy-start(bf16[2304]{0:T(1024)(128)(2,1)} %param.12) | copy-start | bytes 13828
  2.6 0.7 %copy-start.2 = (s32[1,2]{1,0:T(1,128)S(1)}, s32[1,2]{1,0:T(1,128)}, u32[]{:S(2)}) copy-start(s32[1,2]{1,0:T(1,128)} %goal_ref.1) | copy-start | bytes 28

commit v3 on v2

--- a/solution.py
+++ b/solution.py
@@ -86,11 +86,12 @@
         forward_ref, backward_ref, *refs = refs
     kernel_ref, table_ref, carry_h_ref, carry_c_ref, *refs = refs
     if depth:
-        refs, extra = refs[:-14], refs[-14:]
+        refs, extra = refs[:-17], refs[-17:]
         forward_ref, backward_ref, shards, chunks = extra[:4]
         core_land, plane_land, z_sum, z_land = extra[4:8]
-        z_gather, plane_gather, core_gather = extra[8:11]
-        core_scatter, plane_scatter, z_scatter = extra[11:]
+        table_part, table_land = extra[8:10]
+        z_gather, plane_gather, core_gather = extra[10:13]
+        core_scatter, plane_scatter, z_scatter, table_sems = extra[13:]
     (
     fields,
     grads,
@@ -190,7 +191,7 @@
         cells[0, row] = cell_ref[row]
         return 0
 
-    lax.fori_loop(0, row_count, first_row, 0)
+    lax.fori_loop(0, row_count, first_row, 0, unroll=True)
 
 
     def field_copy(step, side):
@@ -280,7 +281,7 @@
             body(row)
             return 0
 
-        lax.fori_loop(low, high, run, 0)
+        lax.fori_loop(low, high, run, 0, unroll=True)
 
     def build_weights():
         flat = jnp.concatenate(
@@ -378,14 +379,38 @@
             lanes = part.shape[1]
             kernel_acc[block, :, :lanes] = kernel_acc[block, :, :lanes] + part
 
+    def start_scatter():
+        chunk_rows = shard_ref.shape[0]
+        half = lax.broadcasted_iota(jnp.int32, (gates // 2, 128), 1) < channels
+        lines = []
+        for pair in range(5):
+            even = kernel_acc[pair, pl.ds(0, gates // 2, stride=2), :]
+            odd = kernel_acc[pair, pl.ds(1, gates // 2, stride=2), :]
+            lines.append(jnp.where(half, even, pltpu.roll(odd, 64, 1)))
+            if pair < 4:
+                lines.append(jnp.where(half, pltpu.roll(even, 64, 1), odd))
+        flat = jnp.concatenate(lines, axis=0)
+        rest = chunks.shape[3] - chunk_rows
+        for index, slot in enumerate(shard_slots(depth)):
+            part = flat[index * chunk_rows : (index + 1) * chunk_rows]
+            chunks[slot] = jnp.concatenate([part, jnp.zeros((rest, 128), jnp.float32)], axis=0)
+        copy = push(chunks.at[1 - core_me], core_land, core_scatter, 0, groups.core_peer())
+        copy.start()
+        return copy
+
     kernel_acc[...] = jnp.zeros(kernel_acc.shape, jnp.float32)
     for step in reversed(range(steps)):
         gate_row(step, 0)
         gate_row(step, row_count - 1)
         send_both(grad_copy, step)
         for_rows(1, row_count - 1, functools.partial(gate_row, step))
-        for_rows(1, row_count - 1, functools.partial(back_row, step))
-        for_rows(0, row_count // 2, lambda pair: kernel_rows(step, 2 * pair))
+        if step:
+            for_rows(1, row_count - 1, functools.partial(back_row, step))
+            for_rows(0, row_count // 2, lambda pair: kernel_rows(step, 2 * pair))
+        else:
+            for_rows(0, row_count // 2, lambda pair: kernel_rows(step, 2 * pair))
+            core_copy = start_scatter() if depth else None
+            for_rows(1, row_count - 1, functools.partial(back_row, step))
         take_grads(step)
         back_row(step, 0)
         back_row(step, row_count - 1)
@@ -412,27 +437,18 @@
         return
 
     chunk_rows = shard_ref.shape[0]
-    half = columns[: gates // 2] < channels
-    lines = []
-    for pair in range(5):
-        even = kernel_acc[pair, pl.ds(0, gates // 2, stride=2), :]
-        odd = kernel_acc[pair, pl.ds(1, gates // 2, stride=2), :]
-        lines.append(jnp.where(half, even, pltpu.roll(odd, 64, 1)))
-        if pair < 4:
-            lines.append(jnp.where(half, pltpu.roll(even, 64, 1), odd))
-    flat = jnp.concatenate(lines, axis=0)
-    rest = chunks.shape[3] - chunk_rows - 3
-    for index, slot in enumerate(shard_slots(depth)):
-        part = flat[index * chunk_rows : (index + 1) * chunk_rows]
-        pieces = [part, flipped[:3]]
-        if rest:
-            pieces.append(jnp.zeros((rest, 128), jnp.float32))
-        chunks[slot] = jnp.concatenate(pieces, axis=0)
-
-    copy = push(chunks.at[1 - core_me], core_land, core_scatter, 0, groups.core_peer())
-    copy.start()
-    copy.wait()
-    chunks[core_me] = chunks[core_me] + core_land[...]
+    table_part[...] = flipped[:8]
+    table_copy = push(table_part, table_land, table_sems, 0, groups.core_peer())
+    table_copy.start()
+    core_copy.wait()
+    table_copy.wait()
+    lines = lax.broadcasted_iota(jnp.int32, (8, 128), 0)
+    pair_table = jnp.where(lines < 3, table_part[...] + table_land[...], 0.0)
+    pad = chunks.shape[3] - chunk_rows - 3
+    placed = jnp.concatenate(
+        [jnp.zeros((chunk_rows, 128), jnp.float32), pair_table[: 3 + pad]], axis=0
+    )
+    chunks[core_me] = chunks[core_me] + core_land[...] + placed
     copies = []
     for step in range(1, 4):
         plane, peer = groups.plane_peer(step)
@@ -507,8 +523,10 @@
             pltpu.VMEM((4, depth, tall, 128), f32),
             pltpu.VMEM((depth, tall, 128), f32),
             pltpu.VMEM((depth, tall, 128), f32),
+            pltpu.VMEM((8, 128), f32),
+            pltpu.VMEM((8, 128), f32),
         ] + [
-            pltpu.SemaphoreType.DMA((2, slots)) for slots in (depth, 4, 1, 1, 4, depth)
+            pltpu.SemaphoreType.DMA((2, slots)) for slots in (depth, 4, 1, 1, 4, depth, 1)
         ]
     grad_kernel, table, carry_h, carry_c = pl.pallas_call(
         functools.partial(main_kernel, depth, scale),

time: 50.8 us -> 48.8 us (0.961)
  Pallas kernels: 44.4 us -> 42.4 us
    pallas_call x1, Pallas kernels: 44.4 us -> 42.4 us  [per_device(): pl.pallas_call(functools.partial(main_kernel, depth, scale), out_shape=(j...]
where the time goes in v3:
time: 48.8 us; the launch traced here: 48.6 us
  Pallas kernels  42.4 us (87%)
  local copies, waits for them, and re-layouts  5.46 us (11%)
  between operations  0.72 us (1%)
    pallas_call x1, Pallas kernels, per_device(): pl.pallas_call(functools.partial(main_kernel, depth, scale), out_shape=(j...  42.4 us
    unnamed x20, local copies, waits for them, and re-layouts  5.46 us

profile of v3, /device:TPU:0, one launch (start us, length us, event | category | flops | bytes accessed | tf_op | source)
XLA Modules:
  0.0 48.6 jit_solution(12788866327579613575)
XLA Ops:
  0.6 0.0 copy-start.5
  0.6 0.0 copy-start.4
  0.7 0.7 %copy-done.5 = f32[3,32]{1,0:T(4,128)S(1)} copy-done((f32[3,32]{1,0:T(4,128)S(1)}, f32[3,32]{1,0:T(4,128)}, u32[]{:S(2)}) %copy-start.5) | copy-done | bytes 408
  1.3 0.1 copy.11
  1.4 0.0 copy-start.3
  1.4 1.0 %copy.22 = bf16[1,32,8,256]{3,1,2,0:T(8,128)(2,1)S(1)} copy(bf16[1,32,8,256]{3,2,1,0:T(8,128)(2,1)} %param.9) | data formatting | bytes 262144 | tf_op args[2]
  2.4 0.0 copy-done.4
  2.4 0.1 copy.21
  2.5 0.0 copy-done.3
  2.5 0.0 copy-start
  2.5 0.0 copy-start.1
  2.5 0.1 copy.20
  2.6 0.0 copy-start.2
  2.6 0.6 %copy-done = s32[1,8,256]{2,1,0:T(8,128)S(1)} copy-done((s32[1,8,256]{2,1,0:T(8,128)S(1)}, s32[1,8,256]{2,1,0:T(8,128)}, u32[]{:S(2)}) %copy-start) | copy-done | bytes 8216
  3.2 0.0 copy-done.1
  3.2 0.1 copy-done.2
  3.3 42.4 %shard_map.102 = (f32[18,128]{1,0:T(8,128)S(1)}, f32[3,32]{1,0:T(4,128)S(1)}, f32[8,32,256]{2,1,0:T(8,128)S(1)}, f32[8,32,256]{2,1,0:T(8,128)S(1)}) custom-call(s32[1,2]{1,0:T(1,128)S(1)} %copy-done.2, s32[8,256]{1,0:T(8,128)S(1)} %bitcast.32, f32[32,3]{1,0:T(8,128)S(1)} %bitcast.30, bf16[8,32,256]{2,1,0:T(8,128)(2,1)S(1)} %bitcast.27, ...), custom_call_target="tpu_custom_call" | custom-call | tf_op jit(solution)/shard_map/pallas_call | solution.py:531
  45.7 0.9 %copy.15 = f32[1,32,8,256]{3,2,1,0:T(8,128)} copy(f32[1,32,8,256]{3,1,2,0:T(8,128)S(1)} %bitcast.29) | data formatting | bytes 524288
  46.5 0.9 %copy.16 = f32[1,32,8,256]{3,2,1,0:T(8,128)} copy(f32[1,32,8,256]{3,1,2,0:T(8,128)S(1)} %bitcast.28) | data formatting | bytes 524288
  47.4 0.6 %copy.25 = f32[2304]{0:T(1024)} copy(f32[2304]{0:T(1024)S(1)} %bitcast.31) | data formatting | bytes 18432
  48.0 0.6 %copy.26 = f32[3,32]{1,0:T(4,128)} copy(f32[3,32]{1,0:T(4,128)S(1)} %get-tuple-element.21) | data formatting | bytes 768
Async XLA Ops:
  0.6 0.7 %copy-start.5 = (f32[3,32]{1,0:T(4,128)S(1)}, f32[3,32]{1,0:T(4,128)}, u32[]{:S(2)}) copy-start(f32[3,32]{1,0:T(4,128)} %param.13) | copy-start | bytes 1156
  0.6 1.7 %copy-start.4 = (f32[1,32,8,256]{3,2,1,0:T(8,128)S(1)}, f32[1,32,8,256]{3,2,1,0:T(8,128)}, u32[]{:S(2)}) copy-start(f32[1,32,8,256]{3,2,1,0:T(8,128)} %param.10) | copy-start | bytes 786436
  1.4 1.1 %copy-start.3 = (bf16[1,3,32,8,256]{4,3,2,1,0:T(8,128)(2,1)S(1)}, bf16[1,3,32,8,256]{4,3,2,1,0:T(8,128)(2,1)}, u32[]{:S(2)}) copy-start(bf16[1,3,32,8,256]{4,3,2,1,0:T(8,128)(2,1)} %param.11) | copy-start | bytes 1179652
  2.5 0.7 %copy-start = (s32[1,8,256]{2,1,0:T(8,128)S(1)}, s32[1,8,256]{2,1,0:T(8,128)}, u32[]{:S(2)}) copy-start(s32[1,8,256]{2,1,0:T(8,128)} %param.7) | copy-start | bytes 24580
  2.5 0.7 %copy-start.1 = (bf16[2304]{0:T(1024)(128)(2,1)S(1)}, bf16[2304]{0:T(1024)(128)(2,1)}, u32[]{:S(2)}) copy-start(bf16[2304]{0:T(1024)(128)(2,1)} %param.12) | copy-start | bytes 13828
  2.6 0.7 %copy-start.2 = (s32[1,2]{1,0:T(1,128)S(1)}, s32[1,2]{1,0:T(1,128)}, u32[]{:S(2)}) copy-start(s32[1,2]{1,0:T(1,128)} %goal_ref.1) | copy-start | bytes 28
